TPU v7x, 128 devices: a whole 4x4x4 slice. The times are simulated.
128 devices in a mesh: rep: 2 (over core), tensor: 64 (over x, z, y).
Axes of the slice: x: 4, y: 4, z: 4, core: 2. Of those that a mesh axis runs over, the one named last changes fastest.
Arguments:
- amplitudes: bfloat16 [4, 1600, 3200], P('rep', 'tensor'), may hold values from -6 to 6
- intermediate: bfloat16 [128, 200, 6400], P('tensor', None, 'rep'), may hold values from -0.21875 to 0.21875
- occ_irrep: int32 [200], replicated, may hold values from 0 to 7
- i_window: int32 [16], replicated, may hold values from 0 to 199
- j_window: int32 [128], replicated, may hold values from 0 to 199
- k_window: int32 [4], replicated, may hold values from 0 to 199
- occ_energy: float32 [200], replicated, may hold values from -1 to -0.3
- virt_energy: float32 [1600], replicated, may hold values from 0.2 to 3
Outputs:
- update: bfloat16 [16, 1600, 25600], P('rep', 'tensor')
Inputs may be any that keep to these rules, and one draw needn't show every extreme that they name: `i_window`: occupied orbital numbers, repeats possible. `j_window`: occupied orbital numbers, repeats possible. `k_window`: occupied orbital numbers, repeats possible.
All inputs are finite; a program needn't handle non-finite values.
Results may differ from a plain program's by a relative error of at most 0.0058.
Values may be sent and summed in bfloat16 or wider, within the bound.
A program may use at most 320 MiB of HBM per device.

v0:
```python
import jax
import jax.numpy as jnp
from jax import lax
from jax.sharding import PartitionSpec as P

IRREPS = 8


def arrange_blocks(w_local, sym_cols, irreps, width):
    n_cols = w_local.shape[0] * w_local.shape[1]
    count = w_local.shape[2] // (irreps * width)
    shaped = w_local.reshape(n_cols, count, irreps, width)
    block_index = jnp.bitwise_xor(jnp.arange(irreps, dtype=jnp.int32)[:, None], sym_cols[None, :])
    k_index = jnp.arange(count, dtype=jnp.int32)[None, :]
    picked = shaped[:, k_index, block_index]
    picked = picked.transpose(1, 2, 3, 0)
    return picked.reshape(irreps, count * width, n_cols)


def block_product(left_rows, right_blocks, first_row, sym_value, width, irreps):
    length = left_rows.shape[0]
    depth = left_rows.shape[1]
    n_cols = right_blocks.shape[2]
    offset = first_row % width
    blocks = (length + 2 * width - 2) // width
    padded = jnp.zeros((blocks * width, depth), left_rows.dtype)
    padded = lax.dynamic_update_slice(padded, left_rows, (offset, jnp.zeros((), offset.dtype)))
    labels = jnp.arange(blocks, dtype=jnp.int32)
    targets = jnp.bitwise_xor(jnp.minimum(labels, irreps - 1), sym_value)
    rights = right_blocks[targets]
    product = jnp.einsum(
        "bwk,bkn->bwn",
        padded.reshape(blocks, width, depth),
        rights,
        preferred_element_type=jnp.float32,
    )
    return lax.dynamic_slice_in_dim(product.reshape(blocks * width, n_cols), offset, length, 0)


def make_worker(arranged, sym_rows, groups, width, irreps):

    def worker(block_rows, first_row):
        k_count = block_rows.shape[0]
        length = block_rows.shape[1]
        members = block_rows.shape[2] // width
        k_step = k_count // groups
        results = []
        for member in range(members):
            member_rows = block_rows[:, :, member * width : (member + 1) * width]
            left_rows = member_rows
            left_rows = left_rows.transpose(1, 0, 2).reshape(length, k_step * width)
            product = block_product(left_rows, arranged, first_row, sym_rows[member], width, irreps)
            summed = lax.optimization_barrier(product.astype(jnp.bfloat16)).astype(jnp.float32)
            results.append(summed.astype(jnp.bfloat16))
        return jnp.stack(results)

    return worker


def per_device(
    amplitudes, intermediate, occ_irrep, i_window, j_window, k_window, occ_energy, virt_energy
):
    irreps = IRREPS
    width = virt_energy.shape[0] // irreps
    batch_i = i_window.shape[0]
    k_local = amplitudes.shape[0]
    replica = lax.axis_index("rep")
    column = lax.axis_index("tensor")
    half_i = batch_i // lax.axis_size("rep")
    own_i = lax.dynamic_slice_in_dim(i_window, replica * half_i, half_i)
    rows_sym = occ_irrep[i_window]
    cols_sym = occ_irrep[lax.dynamic_slice_in_dim(k_window, replica * k_local, k_local)]
    groups = 1
    arranged = arrange_blocks(intermediate, cols_sym, irreps, width)
    worker = make_worker(arranged, rows_sym, groups, width, irreps)
    gathered = worker(lax.all_gather(amplitudes, "tensor", axis=1, tiled=True), jnp.int32(0))
    term = lax.optimization_barrier(gathered).astype(jnp.float32)
    summed = lax.psum_scatter(term.astype(jnp.bfloat16), "rep", scatter_dimension=0, tiled=True)
    returned = lax.all_to_all(summed, "tensor", split_axis=1, concat_axis=2, tiled=True)
    rows_local = returned.shape[1]
    j_total = j_window.shape[0]
    shaped = returned.reshape(half_i, rows_local, j_total, width)
    sym_i = occ_irrep[own_i]
    energy_i = occ_energy[own_i]
    sym_j = occ_irrep[j_window]
    energy_j = occ_energy[j_window]
    energy_a = lax.dynamic_slice_in_dim(virt_energy, column * rows_local, rows_local)
    irrep_a = (column * rows_local + jnp.arange(rows_local, dtype=jnp.int32)) // width
    irrep_b = jnp.bitwise_xor(
        jnp.bitwise_xor(irrep_a[None, :, None], sym_i[:, None, None]), sym_j[None, None, :]
    )
    energy_table = virt_energy.reshape(irreps, width)
    energy_b = jnp.zeros(irrep_b.shape + (width,), jnp.float32)
    for label in range(irreps):
        energy_b = jnp.where(
            irrep_b[..., None] == label, energy_table[label][None, None, None, :], energy_b
        )
    denominator = (
        energy_i[:, None, None, None]
        + energy_j[None, None, :, None]
        - energy_a[None, :, None, None]
        - energy_b
    )
    result = (shaped.astype(jnp.float32) / denominator).astype(jnp.bfloat16)
    return result.reshape(half_i, rows_local, j_total * width)


def solution(mesh):
    return jax.shard_map(
        per_device,
        mesh=mesh,
        in_specs=(P("rep", "tensor", None), P("tensor", None, "rep"), P(), P(), P(), P(), P(), P()),
        out_specs=P("rep", "tensor", None),
        check_vma=False,
    )
```

profile of v0, /device:TPU:1, one launch (start us, length us, event | category | flops | bytes accessed | tf_op | source)
XLA Modules:
  0.0 842.1 jit_solution(1066107681700497681)
XLA Ops:
  10.1 11.8 %reshape.557 = bf16[400,2,8,200]{3,2,1,0:T(8,128)(2,1)} reshape(bf16[2,200,3200]{2,1,0:T(8,128)(2,1)} %param.9) | data formatting | bytes 5120000 | tf_op jit(solution)/shard_map/reshape | solution.py:12
  21.9 3.1 copy.67
  27.5 5.1 copy.68
  41.7 3.0 gather_fusion.5
  90.1 39.3 %all-gather.2.cloned.1.call-done = bf16[2,1600,3200]{2,0,1:T(2,128)(2,1)} async-done(((bf16[2,25,3200]{2,0,1:T(2,128)(2,1)}), bf16[2,1600,3200]{2,0,1:T(2,128)(2,1)}) %all-gather.2.cloned.1.call-update) | async-done | bytes 20480016 | tf_op jit(solution)/shard_map/all_gather | solution.py:76
  129.4 46.7 %fusion.19 = (bf16[2,1600,200]{2,0,1:T(2,128)(2,1)S(1)}, bf16[2,1600,200]{2,0,1:T(2,128)(2,1)}, bf16[2,1600,200]{2,0,1:T(2,128)(2,1)}, bf16[2,1600,200]{2,0,1:T(...) fusion(bf16[2,1600,3200]{2,0,1:T(2,128)(2,1)} %all-gather.2.clo, ...), kind=kLoop, calls=%fused_computation.130 | loop fusion | bytes 40960000 | tf_op jit(solution)/shard_map/slice | solution.py:49
  176.2 3.9 copy.117
  183.0 3.2 fusion.22
  191.2 3.8 copy.118
  197.9 3.2 fusion.23
  203.5 5.3 copy.119
  211.7 3.2 fusion.24
  217.3 5.3 copy.120
  225.6 3.2 fusion.25
  231.2 5.4 copy.121
  239.7 3.2 fusion.26
  245.3 5.3 copy.122
  253.6 3.2 fusion.27
  259.3 5.3 copy.123
  267.5 3.2 fusion.28
  273.2 5.3 copy.124
  281.4 3.2 fusion.29
  287.0 5.3 copy.125
  295.3 3.2 fusion.30
  301.0 5.3 copy.126
  309.3 3.2 fusion.31
  314.9 5.3 copy.127
  320.2 3.1 copy.143
  323.6 3.2 fusion.32
  329.2 5.4 copy.128
  337.5 3.2 fusion.33
  343.2 5.3 copy.129
  351.5 3.2 fusion.34
  357.2 5.3 copy.130
  365.4 3.2 fusion.35
  371.2 5.3 copy.131
  379.5 3.2 fusion.36
  385.1 3.9 copy.132
  391.9 3.2 fusion.37
  416.3 33.4 %reduce-scatter.5.cloned.1.call-done = bf16[8,1600,400]{1,2,0:T(8,128)(2,1)} async-done(((bf16[16,1600,400]{1,2,0:T(8,128)(2,1)}), bf16[8,1600,400]{1,2,0:T(8,128)(2,1)}) %reduce-scatter.5.cloned.1.call-update) | async-done | bytes 10240016
  449.7 20.0 %copy.115 = bf16[8,1600,400]{2,0,1:T(8,128)(2,1)} copy(bf16[8,1600,400]{1,2,0:T(8,128)(2,1)} %reduce-scatter.5.cloned.1.call-done) | data formatting | bytes 20480000 | tf_op jit(solution)/shard_map/reduce_scatter | solution.py:78
  469.6 10.5 %all-to-all-start = ((bf16[8,1600,400]{2,0,1:T(8,128)(2,1)}), bf16[8,1600,400]{2,0,1:T(8,128)(2,1)}, u32[]{:S(2)}, u32[]{:S(2)}) async-start(bf16[8,1600,400]{2,0,1:T(8,128)(2,1)} %copy.115), calls=%async_computation | async-start | bytes 26214400 | tf_op jit(solution)/shard_map/all_to_all | solution.py:79
  484.4 9.1 %sub.36 = f32[8,25,128,200]{3,2,0,1:T(8,128)} broadcast(f32[8,25,128]{2,0,1:T(8,128)S(1)} %broadcast_subtract_fusion), dimensions={0,1,2} | broadcast | bytes 20582400 | tf_op jit(solution)/shard_map/sub | solution.py:99
  493.4 25.1 %sub.37 = f32[8,25,25600]{2,0,1:T(8,128)} reshape(f32[8,25,128,200]{3,2,0,1:T(8,128)} %sub.36) | data formatting | bytes 40960000 | tf_op jit(solution)/shard_map/sub | solution.py:99
  518.8 5.6 broadcast_in_dim.195
  524.4 23.6 %broadcast_in_dim.196 = pred[8,25,25600]{2,0,1:T(8,128)(4,1)} reshape(pred[8,25,128,200]{3,2,0,1:T(8,128)(4,1)} %broadcast_in_dim.195) | data formatting | bytes 10240000 | tf_op jit(solution)/shard_map/jit(_where)/broadcast_in_dim | solution.py:95
  548.0 5.5 broadcast_in_dim.200
  553.5 23.6 %broadcast_in_dim.201 = pred[8,25,25600]{2,0,1:T(8,128)(4,1)} reshape(pred[8,25,128,200]{3,2,0,1:T(8,128)(4,1)} %broadcast_in_dim.200) | data formatting | bytes 10240000 | tf_op jit(solution)/shard_map/jit(_where)/broadcast_in_dim | solution.py:95
  577.1 5.5 broadcast_in_dim.205
  582.6 23.8 %broadcast_in_dim.206 = pred[8,25,25600]{2,0,1:T(8,128)(4,1)} reshape(pred[8,25,128,200]{3,2,0,1:T(8,128)(4,1)} %broadcast_in_dim.205) | data formatting | bytes 10240000 | tf_op jit(solution)/shard_map/jit(_where)/broadcast_in_dim | solution.py:95
  606.4 5.5 broadcast_in_dim.210
  611.9 23.6 %broadcast_in_dim.211 = pred[8,25,25600]{2,0,1:T(8,128)(4,1)} reshape(pred[8,25,128,200]{3,2,0,1:T(8,128)(4,1)} %broadcast_in_dim.210) | data formatting | bytes 10240000 | tf_op jit(solution)/shard_map/jit(_where)/broadcast_in_dim | solution.py:95
  635.5 5.5 broadcast_in_dim.215
  640.9 23.6 %broadcast_in_dim.216 = pred[8,25,25600]{2,0,1:T(8,128)(4,1)} reshape(pred[8,25,128,200]{3,2,0,1:T(8,128)(4,1)} %broadcast_in_dim.215) | data formatting | bytes 10240000 | tf_op jit(solution)/shard_map/jit(_where)/broadcast_in_dim | solution.py:95
  664.5 5.5 broadcast_in_dim.220
  670.0 23.6 %broadcast_in_dim.221 = pred[8,25,25600]{2,0,1:T(8,128)(4,1)} reshape(pred[8,25,128,200]{3,2,0,1:T(8,128)(4,1)} %broadcast_in_dim.220) | data formatting | bytes 10240000 | tf_op jit(solution)/shard_map/jit(_where)/broadcast_in_dim | solution.py:95
  693.6 5.5 broadcast_in_dim.225
  699.1 24.0 %broadcast_in_dim.226 = pred[8,25,25600]{2,0,1:T(8,128)(4,1)} reshape(pred[8,25,128,200]{3,2,0,1:T(8,128)(4,1)} %broadcast_in_dim.225) | data formatting | bytes 10240000 | tf_op jit(solution)/shard_map/jit(_where)/broadcast_in_dim | solution.py:95
  723.1 5.5 broadcast_in_dim.230
  728.6 23.6 %broadcast_in_dim.231 = pred[8,25,25600]{2,0,1:T(8,128)(4,1)} reshape(pred[8,25,128,200]{3,2,0,1:T(8,128)(4,1)} %broadcast_in_dim.230) | data formatting | bytes 10240000 | tf_op jit(solution)/shard_map/jit(_where)/broadcast_in_dim | solution.py:95
  753.6 7.6 convert_bitcast_fusion
  761.2 17.6 %copy.116 = f32[8,25,64,400]{3,2,0,1:T(8,128)} copy(f32[8,25,64,400]{3,0,1,2:T(8,128)S(1)} %convert_bitcast_fusion) | data formatting | bytes 40960000 | tf_op jit(solution)/shard_map/convert_element_type | solution.py:104
  778.8 23.7 %reshape.589 = f32[8,25,25600]{2,0,1:T(8,128)} reshape(f32[8,25,64,400]{3,2,0,1:T(8,128)} %copy.116) | data formatting | bytes 40960000 | tf_op jit(solution)/shard_map/convert_element_type | solution.py:104
  802.5 32.6 %divide_convert_fusion = bf16[8,25,25600]{2,0,1:T(8,128)(2,1)} fusion(f32[8,25,25600]{2,0,1:T(8,128)} %reshape.589, f32[8,25,25600]{2,0,1:T(8,128)} %sub.37, pred[8,25,25600]{2,0,1:T(8,128)(4,1)} %broadcast_in_dim.196, pred[8,25,25600]{2,0,1:T(8,128)(4,1)} %broadcast_in_dim.201, pred[8,25,25600]{2,0,1:T(8,128)(4,1)} %broadcast_in_dim.206, ...), kind=kLoop, calls=%fused_computation.24 | loop fusion | flops 56320000 | bytes 92979200 | tf_op jit(solution)/shard_map/convert_element_type | solution.py:104
  (205 shorter events, 171.2 us)
Async XLA Ops:
  6.5 1.4 copy-start
  6.5 122.9 %all-gather.2.cloned.1.call-start = ((), (), s32[]{:S(2)}) async-start(), calls=%async_computation.2 | async-start | bytes 20800000 | tf_op jit(solution)/shard_map/all_gather | solution.py:76
  7.3 442.4 %reduce-scatter.5.cloned.1.call-start = ((), (), s32[]{:S(2)}) async-start(), calls=%async_computation.3 | async-start | bytes 31948800
  188.6 2.6 copy-start.2
  395.1 2.6 copy-start.3
  397.7 1.8 copy-start.4
  397.7 3.0 copy-start.5
  399.5 2.4 copy-start.6
  400.7 2.4 copy-start.7
  401.9 2.4 copy-start.8
  403.1 2.5 copy-start.9
  404.3 2.4 copy-start.10
  405.6 2.3 copy-start.11
  406.7 2.4 copy-start.12
  407.9 2.4 copy-start.13
  409.1 2.4 copy-start.14
  410.3 2.3 copy-start.15
  411.5 2.4 copy-start.16
  412.7 2.4 copy-start.17
  469.6 10.5 %copy-start.19 = (s32[16]{0:T(128)S(1)}, s32[16]{0:T(128)}, u32[]{:S(2)}) copy-start(s32[16]{0:T(128)} %param.11) | copy-start | bytes 196
  469.6 10.6 %copy-start.20 = (s32[128]{0:T(128)S(1)}, s32[128]{0:T(128)}, u32[]{:S(2)}) copy-start(s32[128]{0:T(128)} %param.12) | copy-start | bytes 1540
  469.6 11.3 %copy-start.1 = (f32[200]{0:T(256)S(1)}, f32[200]{0:T(256)}, u32[]{:S(2)}) copy-start(f32[200]{0:T(256)} %param.14) | copy-start | bytes 2404
  469.6 14.5 %copy-start.18 = (f32[1600]{0:T(1024)S(1)}, f32[1600]{0:T(1024)}, u32[]{:S(2)}) copy-start(f32[1600]{0:T(1024)} %param.15) | copy-start | bytes 19204
  469.6 283.9 %all-to-all-start = ((bf16[8,1600,400]{2,0,1:T(8,128)(2,1)}), bf16[8,1600,400]{2,0,1:T(8,128)(2,1)}, u32[]{:S(2)}, u32[]{:S(2)}) async-start(bf16[8,1600,400]{2,0,1:T(8,128)(2,1)} %copy.115), calls=%async_computation | async-start | bytes 26214400 | tf_op jit(solution)/shard_map/all_to_all | solution.py:79
Sparse Core Ops, SparseCore 0:
  10.2 119.1 all-gather.1
  416.4 33.2 reduce-scatter.4
where the time goes:
time: 851 us; the launch traced here: 842 us
  local copies, waits for them, and re-layouts  641 us (75%)
  waiting for transfers between devices  73.5 us (9%)
  other arithmetic  52.4 us (6%)
  matrix products  50.6 us (6%)
  between operations  14.5 us (2%)
  starting transfers between devices  10.5 us (1%)
    broadcast_in_dim x32, local copies, waits for them, and re-layouts, per_device(): jnp.where(irrep_b[..., None] == label, energy_table[label][None, None, No...  235 us
    unnamed x89, local copies, waits for them, and re-layouts  145 us
    dot_general x16, matrix products, block_product(): jnp.einsum('bwk,bkn->bwn', padded.reshape(blocks, width, depth), rights,...  50.6 us
    slice x1, local copies, waits for them, and re-layouts, worker(): member_rows = block_rows[:, :, member * width:(member + 1) * width]  46.7 us
    gather x16, local copies, waits for them, and re-layouts, block_product(): rights = right_blocks[targets]  46.3 us
    convert_element_type x2, local copies, waits for them, and re-layouts, per_device(): result = (shaped.astype(jnp.float32) / denominator).astype(jnp.bfloat16)  41.3 us
    convert_element_type x2, other arithmetic, per_device(): result = (shaped.astype(jnp.float32) / denominator).astype(jnp.bfloat16)  40.2 us
    all_gather x1, waiting for transfers between devices, per_device(): lax.all_gather(amplitudes, 'tensor', axis=1, tiled=True)  39.3 us
  transfers between devices with their start and end apart: 3, of which 2 were waited for; matrix products, arithmetic and copies ran while one was open for 42% of the time, Pallas kernels for 0%

commit v1 on v0

--- a/solution.py
+++ b/solution.py
@@ -1,9 +1,20 @@
+import functools
 import jax
 import jax.numpy as jnp
 from jax import lax
 from jax.sharding import PartitionSpec as P
 
 IRREPS = 8
+
+
+def _divide_tasks(local_x, which_axis):
+    carry_in = tuple((local_x for _ in range(lax.axis_size(which_axis))))
+    side_arr = jnp.stack(carry_in, 0)
+    b_next = lax.all_to_all(side_arr, which_axis, split_axis=0, concat_axis=0)
+    return jnp.concatenate(b_next, 1)
+
+
+replace_desk_now = functools.partial(_divide_tasks, which_axis="tensor")
 
 
 def arrange_blocks(w_local, sym_cols, irreps, width):
@@ -73,7 +84,7 @@
     groups = 1
     arranged = arrange_blocks(intermediate, cols_sym, irreps, width)
     worker = make_worker(arranged, rows_sym, groups, width, irreps)
-    gathered = worker(lax.all_gather(amplitudes, "tensor", axis=1, tiled=True), jnp.int32(0))
+    gathered = worker(replace_desk_now(amplitudes), jnp.int32(0))
     term = lax.optimization_barrier(gathered).astype(jnp.float32)
     summed = lax.psum_scatter(term.astype(jnp.bfloat16), "rep", scatter_dimension=0, tiled=True)
     returned = lax.all_to_all(summed, "tensor", split_axis=1, concat_axis=2, tiled=True)

time: 851 us -> 1150 us (1.35)
  waiting for transfers between devices: 73.5 us -> 346 us
  starting transfers between devices: 10.5 us -> 22.9 us
  local copies, waits for them, and re-layouts: 641 us -> 653 us
    all_to_all x0 -> x1, waiting for transfers between devices: none -> 257 us  [_divide_tasks(): b_next = lax.all_to_all(side_arr, which_axis, split_axis=0, concat_axis=0)]
    transpose x0 -> x17, local copies, waits for them, and re-layouts: none -> 128 us  [worker(): left_rows = left_rows.transpose(1, 0, 2).reshape(length, k_step * width)]
    unnamed x89 -> x79, local copies, waits for them, and re-layouts: 145 us -> 63.8 us
    unnamed x3 -> x2, waiting for transfers between devices: 34.1 us -> 88.9 us
    slice x1 -> x0, local copies, waits for them, and re-layouts: 46.7 us -> none  [worker(): member_rows = block_rows[:, :, member * width:(member + 1) * width]]
    all_gather x1 -> x0, waiting for transfers between devices: 39.3 us -> none  [per_device(): lax.all_gather(amplitudes, 'tensor', axis=1, tiled=True)]
    another operation x0 -> x1, local copies, waits for them, and re-layouts: none -> 13.9 us  [_divide_tasks(): side_arr = jnp.stack(carry_in, 0)]
    all_to_all x0 -> x1, starting transfers between devices: none -> 12.3 us  [_divide_tasks(): b_next = lax.all_to_all(side_arr, which_axis, split_axis=0, concat_axis=0)]
  transfers between devices with their start and end apart: 3 -> 3, of which waited for: 2 -> 2; matrix products, arithmetic and copies ran while one was open for 42% -> 31% of each run, Pallas kernels for 0% -> 0%
where the time goes in v1:
time: 1150 us; the launch traced here: 1140 us
  local copies, waits for them, and re-layouts  653 us (57%)
  waiting for transfers between devices  346 us (30%)
  other arithmetic  50.9 us (4%)
  matrix products  50.6 us (4%)
  starting transfers between devices  22.9 us (2%)
  between operations  14.6 us (1%)
    all_to_all x1, waiting for transfers between devices, _divide_tasks(): b_next = lax.all_to_all(side_arr, which_axis, split_axis=0, concat_axis=0)  257 us
    broadcast_in_dim x32, local copies, waits for them, and re-layouts, per_device(): jnp.where(irrep_b[..., None] == label, energy_table[label][None, None, No...  235 us
    transpose x17, local copies, waits for them, and re-layouts, worker(): left_rows = left_rows.transpose(1, 0, 2).reshape(length, k_step * width)  128 us
    unnamed x2, waiting for transfers between devices  88.9 us
    unnamed x79, local copies, waits for them, and re-layouts  63.8 us
    dot_general x16, matrix products, block_product(): jnp.einsum('bwk,bkn->bwn', padded.reshape(blocks, width, depth), rights,...  50.6 us
    gather x16, local copies, waits for them, and re-layouts, block_product(): rights = right_blocks[targets]  46.4 us
    convert_element_type x2, local copies, waits for them, and re-layouts, per_device(): result = (shaped.astype(jnp.float32) / denominator).astype(jnp.bfloat16)  41.4 us
  transfers between devices with their start and end apart: 3, of which 2 were waited for; matrix products, arithmetic and copies ran while one was open for 31% of the time, Pallas kernels for 0%

profile of v1, /device:TPU:1, one launch (start us, length us, event | category | flops | bytes accessed | tf_op | source)
XLA Modules:
  0.0 1137.9 jit_solution(9655102654821938290)
XLA Ops:
  6.5 13.9 %stack.36 = bf16[64,2,25,3200]{3,1,2,0:T(2,128)(2,1)} broadcast(bf16[2,25,3200]{2,0,1:T(2,128)(2,1)} %param.8), dimensions={1,2,3} | broadcast | bytes 20800000 | tf_op jit(solution)/shard_map/stack | solution.py:12
  20.4 12.3 %all-to-all-start = ((bf16[64,2,25,3200]{3,1,2,0:T(2,128)(2,1)}), bf16[64,2,25,3200]{3,1,2,0:T(2,128)(2,1)}, u32[]{:S(2)}, u32[]{:S(2)}) async-start(bf16[64,2,25,3200]{3,1,2,0:T(2,128)(2,1)} %stack.36), calls=%async_computation | async-start | bytes 40960000 | tf_op jit(solution)/shard_map/all_to_all | solution.py:13
  34.4 10.7 reshape.567
  50.5 4.7 copy.83
  112.6 257.1 %all-to-all-done = bf16[64,2,25,3200]{3,1,2,0:T(2,128)(2,1)} async-done(((bf16[64,2,25,3200]{3,1,2,0:T(2,128)(2,1)}), bf16[64,2,25,3200]{3,1,2,0:T(2,128)(2,1)}, u32[]{:S(2)}, u32[]{:S(2)}) %all-to-all-start) | async-done | bytes 20480032 | tf_op jit(solution)/shard_map/all_to_all | solution.py:13
  369.7 46.8 %slice_bitcast_fusion = (bf16[1600,2,200]{2,1,0:T(2,128)(2,1)S(1)}, bf16[1600,2,200]{2,1,0:T(2,128)(2,1)}, bf16[1600,2,200]{2,1,0:T(2,128)(2,1)}, bf16[1600,2,20...) fusion(bf16[2,1600,3200]{2,0,1:T(2,128)(2,1)} %bitcast.1), kind=kLoop, calls=%fused_computation.41 | loop fusion | bytes 40960000 | tf_op jit(solution)/shard_map/transpose | solution.py:62
  416.5 3.9 copy.80
  423.3 3.2 fusion.21
  431.6 3.8 copy.85
  438.3 3.2 fusion.22
  443.8 5.3 copy.88
  452.1 3.2 fusion.23
  457.7 5.4 copy.91
  466.0 3.2 fusion.24
  471.7 5.4 copy.94
  477.1 3.1 copy.136
  480.4 3.2 fusion.25
  486.0 5.3 copy.97
  494.2 3.2 fusion.26
  499.9 5.3 copy.100
  508.1 3.2 fusion.27
  513.7 5.3 copy.103
  522.0 3.2 fusion.28
  527.6 5.3 copy.106
  535.9 3.2 fusion.29
  541.5 5.3 copy.109
  549.8 3.2 fusion.30
  555.4 5.3 copy.112
  563.8 3.2 fusion.31
  569.5 5.4 copy.115
  577.8 3.2 fusion.32
  583.5 5.3 copy.118
  591.7 3.2 fusion.33
  597.4 5.4 copy.121
  605.7 3.2 fusion.34
  611.3 5.3 copy.124
  619.5 3.2 fusion.35
  625.1 3.9 copy.127
  632.0 3.2 fusion.36
  656.5 88.9 %reduce-scatter.5.cloned.1.call-done = bf16[8,1600,400]{1,2,0:T(8,128)(2,1)} async-done(((bf16[16,1600,400]{1,2,0:T(8,128)(2,1)}), bf16[8,1600,400]{1,2,0:T(8,128)(2,1)}) %reduce-scatter.5.cloned.1.call-update) | async-done | bytes 10240016
  745.4 20.0 %copy.130 = bf16[8,1600,400]{2,0,1:T(8,128)(2,1)} copy(bf16[8,1600,400]{1,2,0:T(8,128)(2,1)} %reduce-scatter.5.cloned.1.call-done) | data formatting | bytes 20480000 | tf_op jit(solution)/shard_map/reduce_scatter | solution.py:89
  765.4 10.5 all-to-all-start.1
  780.1 9.0 sub.36
  789.2 25.1 %sub.37 = f32[8,25,25600]{2,0,1:T(8,128)} reshape(f32[8,25,128,200]{3,2,0,1:T(8,128)} %sub.36) | data formatting | bytes 40960000 | tf_op jit(solution)/shard_map/sub | solution.py:110
  814.5 5.6 broadcast_in_dim.195
  820.1 23.6 %broadcast_in_dim.196 = pred[8,25,25600]{2,0,1:T(8,128)(4,1)} reshape(pred[8,25,128,200]{3,2,0,1:T(8,128)(4,1)} %broadcast_in_dim.195) | data formatting | bytes 10240000 | tf_op jit(solution)/shard_map/jit(_where)/broadcast_in_dim | solution.py:106
  843.7 5.5 broadcast_in_dim.200
  849.2 23.6 %broadcast_in_dim.201 = pred[8,25,25600]{2,0,1:T(8,128)(4,1)} reshape(pred[8,25,128,200]{3,2,0,1:T(8,128)(4,1)} %broadcast_in_dim.200) | data formatting | bytes 10240000 | tf_op jit(solution)/shard_map/jit(_where)/broadcast_in_dim | solution.py:106
  872.8 5.5 broadcast_in_dim.205
  878.3 24.0 %broadcast_in_dim.206 = pred[8,25,25600]{2,0,1:T(8,128)(4,1)} reshape(pred[8,25,128,200]{3,2,0,1:T(8,128)(4,1)} %broadcast_in_dim.205) | data formatting | bytes 10240000 | tf_op jit(solution)/shard_map/jit(_where)/broadcast_in_dim | solution.py:106
  902.3 5.5 broadcast_in_dim.210
  907.8 23.6 %broadcast_in_dim.211 = pred[8,25,25600]{2,0,1:T(8,128)(4,1)} reshape(pred[8,25,128,200]{3,2,0,1:T(8,128)(4,1)} %broadcast_in_dim.210) | data formatting | bytes 10240000 | tf_op jit(solution)/shard_map/jit(_where)/broadcast_in_dim | solution.py:106
  931.4 5.5 broadcast_in_dim.215
  936.9 23.6 %broadcast_in_dim.216 = pred[8,25,25600]{2,0,1:T(8,128)(4,1)} reshape(pred[8,25,128,200]{3,2,0,1:T(8,128)(4,1)} %broadcast_in_dim.215) | data formatting | bytes 10240000 | tf_op jit(solution)/shard_map/jit(_where)/broadcast_in_dim | solution.py:106
  960.5 5.5 broadcast_in_dim.220
  966.0 23.6 %broadcast_in_dim.221 = pred[8,25,25600]{2,0,1:T(8,128)(4,1)} reshape(pred[8,25,128,200]{3,2,0,1:T(8,128)(4,1)} %broadcast_in_dim.220) | data formatting | bytes 10240000 | tf_op jit(solution)/shard_map/jit(_where)/broadcast_in_dim | solution.py:106
  989.6 5.5 broadcast_in_dim.225
  995.1 23.7 %broadcast_in_dim.226 = pred[8,25,25600]{2,0,1:T(8,128)(4,1)} reshape(pred[8,25,128,200]{3,2,0,1:T(8,128)(4,1)} %broadcast_in_dim.225) | data formatting | bytes 10240000 | tf_op jit(solution)/shard_map/jit(_where)/broadcast_in_dim | solution.py:106
  1018.8 5.5 broadcast_in_dim.230
  1024.3 23.6 %broadcast_in_dim.231 = pred[8,25,25600]{2,0,1:T(8,128)(4,1)} reshape(pred[8,25,128,200]{3,2,0,1:T(8,128)(4,1)} %broadcast_in_dim.230) | data formatting | bytes 10240000 | tf_op jit(solution)/shard_map/jit(_where)/broadcast_in_dim | solution.py:106
  1049.3 7.6 convert_bitcast_fusion
  1056.9 17.6 %copy.131 = f32[8,25,64,400]{3,2,0,1:T(8,128)} copy(f32[8,25,64,400]{3,0,1,2:T(8,128)S(1)} %convert_bitcast_fusion) | data formatting | bytes 40960000 | tf_op jit(solution)/shard_map/convert_element_type | solution.py:115
  1074.5 23.7 %reshape.599 = f32[8,25,25600]{2,0,1:T(8,128)} reshape(f32[8,25,64,400]{3,2,0,1:T(8,128)} %copy.131) | data formatting | bytes 40960000 | tf_op jit(solution)/shard_map/convert_element_type | solution.py:115
  1098.2 32.6 %divide_convert_fusion = bf16[8,25,25600]{2,0,1:T(8,128)(2,1)} fusion(f32[8,25,25600]{2,0,1:T(8,128)} %reshape.599, f32[8,25,25600]{2,0,1:T(8,128)} %sub.37, pred[8,25,25600]{2,0,1:T(8,128)(4,1)} %broadcast_in_dim.196, pred[8,25,25600]{2,0,1:T(8,128)(4,1)} %broadcast_in_dim.201, pred[8,25,25600]{2,0,1:T(8,128)(4,1)} %broadcast_in_dim.206, ...), kind=kLoop, calls=%fused_computation.24 | loop fusion | flops 56320000 | bytes 92979200 | tf_op jit(solution)/shard_map/convert_element_type | solution.py:115
  (211 shorter events, 174.9 us)
Async XLA Ops:
  6.5 26.3 %copy-start = (s32[200]{0:T(256)S(1)}, s32[200]{0:T(256)}, u32[]{:S(2)}) copy-start(s32[200]{0:T(256)} %param.10) | copy-start | bytes 2404
  20.4 12.4 %copy-start.21 = (s32[16]{0:T(128)S(1)}, s32[16]{0:T(128)}, u32[]{:S(2)}) copy-start(s32[16]{0:T(128)} %param.11) | copy-start | bytes 196
  20.4 13.1 %copy-start.20 = (s32[4]{0:T(128)S(1)}, s32[4]{0:T(128)}, u32[]{:S(2)}) copy-start(s32[4]{0:T(128)} %param.13) | copy-start | bytes 52
  20.4 14.0 %copy-start.18 = (bf16[2,200,3200]{2,1,0:T(8,128)(2,1)S(1)}, bf16[2,200,3200]{2,1,0:T(8,128)(2,1)}, u32[]{:S(2)}) copy-start(bf16[2,200,3200]{2,1,0:T(8,128)(2,1)} %param.9) | copy-start | bytes 7680004
  20.4 349.3 %all-to-all-start = ((bf16[64,2,25,3200]{3,1,2,0:T(2,128)(2,1)}), bf16[64,2,25,3200]{3,1,2,0:T(2,128)(2,1)}, u32[]{:S(2)}, u32[]{:S(2)}) async-start(bf16[64,2,25,3200]{3,1,2,0:T(2,128)(2,1)} %stack.36), calls=%async_computation | async-start | bytes 40960000 | tf_op jit(solution)/shard_map/all_to_all | solution.py:13
  32.8 712.6 %reduce-scatter.5.cloned.1.call-start = ((), (), s32[]{:S(2)}) async-start(), calls=%async_computation.3 | async-start | bytes 31948800
  428.9 2.7 copy-start.2
  635.1 2.8 copy-start.3
  637.9 1.8 copy-start.4
  637.9 3.0 copy-start.5
  639.7 2.4 copy-start.6
  640.9 2.4 copy-start.7
  642.1 2.4 copy-start.8
  643.3 2.5 copy-start.9
  644.6 2.4 copy-start.10
  645.8 2.3 copy-start.11
  647.0 2.4 copy-start.12
  648.1 2.4 copy-start.13
  649.4 2.4 copy-start.14
  650.6 2.4 copy-start.15
  651.8 2.4 copy-start.16
  652.9 2.4 copy-start.17
  765.4 10.5 copy-start.22
  765.4 10.6 copy-start.23
  765.4 11.3 copy-start.1
  765.4 14.5 %copy-start.19 = (f32[1600]{0:T(1024)S(1)}, f32[1600]{0:T(1024)}, u32[]{:S(2)}) copy-start(f32[1600]{0:T(1024)} %param.15) | copy-start | bytes 19204
  765.4 283.9 %all-to-all-start.1 = ((bf16[8,1600,400]{2,0,1:T(8,128)(2,1)}), bf16[8,1600,400]{2,0,1:T(8,128)(2,1)}, u32[]{:S(2)}, u32[]{:S(2)}) async-start(bf16[8,1600,400]{2,0,1:T(8,128)(2,1)} %copy.130), calls=%async_computation.1 | async-start | bytes 26214400 | tf_op jit(solution)/shard_map/all_to_all | solution.py:90
Sparse Core Ops, SparseCore 0:
  656.7 88.6 reduce-scatter.4
